TPU v7x, 32 devices: a whole 2x2x4 slice. The times are simulated.
32 devices in a mesh: sample: 4 (over y, x), fsdp: 8 (over z, core).
Axes of the slice: x: 2, y: 2, z: 4, core: 2. Of those that a mesh axis runs over, the one named last changes fastest.
Arguments:
- seed_step: int32 [2], replicated, may hold values from 0 to 16777215
- attn: bfloat16 [16384, 2048], P(('sample', 'fsdp')), may hold values from -6 to 6
- resid: bfloat16 [16384, 4096], P(('sample', 'fsdp')), may hold values from -36 to 36
- cotangent: bfloat16 [16384, 4096], P(('sample', 'fsdp')), may hold values from -6 to 6
- gain: bfloat16 [4096], replicated, may hold values from 0.099609375 to 1.8984375
- mean: float32 [2048, 4096], P('fsdp'), may hold values from -6 to 6
- hess: float32 [2048, 4096], P('fsdp'), may hold values from 0.25 to 4
- momentum: float32 [2048, 4096], P('fsdp'), may hold values from -3 to 3
Outputs:
- new_mean: float32 [2048, 4096], P('fsdp')
- new_hess: float32 [2048, 4096], P('fsdp')
- new_momentum: float32 [2048, 4096], P('fsdp')
All inputs are finite; a program needn't handle non-finite values.
Results may differ from a plain program's by a relative error of at most 0.0035.
Values may be sent and summed in bfloat16 or wider, within the bound.
A program may use at most 192 MiB of HBM per device.

v0:
```python
import jax
import jax.numpy as jnp
from jax import lax
from jax.sharding import PartitionSpec as P

ess_value = 10.0
decay_first = 0.8
decay_second = 0.8
step_size = 0.3
damping = 0.1
norm_eps = 1e-05


def noise_table(seed_step, group_id, row_start, row_count, in_width, width):
    row_index = jnp.arange(row_count, dtype=jnp.int32)[:, None] + row_start
    col_index = jnp.arange(width, dtype=jnp.int32)[None, :]
    mixing = (group_id * in_width + row_index) * width + col_index
    mixing = jnp.bitwise_xor(mixing, seed_step[0])
    mixing = mixing * 668265261 + seed_step[1] * 374761393
    mixing = jnp.bitwise_xor(mixing, jnp.right_shift(mixing, 15) & 131071)
    mixing = mixing * 739982445
    mixing = jnp.bitwise_xor(mixing, jnp.right_shift(mixing, 12) & 1048575)
    mixing = mixing * 695872825
    mixing = jnp.bitwise_xor(mixing, jnp.right_shift(mixing, 15) & 131071)
    first_unif = ((mixing & 4095).astype(jnp.float32) + 0.5) / 4096.0
    second_unif = ((jnp.right_shift(mixing, 12) & 4095).astype(jnp.float32) + 0.5) / 4096.0
    return 2.449489742783178 * (first_unif + second_unif - 1.0)


def ivon_update(mean, hess, momentum, grad_sum, curv_sum, groups):
    grad_mean = grad_sum / groups
    hess_est = curv_sum / groups
    new_momentum = decay_first * momentum + (1.0 - decay_first) * grad_mean
    new_hess = (
        decay_second * hess
        + (1.0 - decay_second) * hess_est
        + 0.5 * (1.0 - decay_second) ** 2 * (hess - hess_est) ** 2 / (hess + damping)
    )
    new_mean = mean - step_size * (new_momentum + damping * mean) / (new_hess + damping)
    return (new_mean, new_hess, new_momentum)


def per_device(seed_step, attn, resid, cotangent, gain, mean, hess, momentum):
    own_rows = mean.shape[0]
    width = mean.shape[1]
    in_width = attn.shape[1]
    scaling = in_width ** (-0.5)
    groups = lax.axis_size("sample")
    group_id = lax.axis_index("sample")
    shard_id = lax.axis_index("fsdp")
    sigma = 1.0 / jnp.sqrt(ess_value * (hess + damping))
    epsilon = noise_table(seed_step, group_id, shard_id * own_rows, own_rows, in_width, width)
    sampled = (
        mean.astype(jnp.bfloat16).astype(jnp.float32)
        + sigma.astype(jnp.bfloat16).astype(jnp.float32) * epsilon
    ).astype(jnp.bfloat16)
    columns = attn
    product = jnp.dot(
        columns,
        lax.all_gather(sampled, "fsdp", axis=0, tiled=True),
        preferred_element_type=jnp.float32,
    )
    total = resid.astype(jnp.float32) + product * scaling
    inverse = lax.rsqrt(jnp.mean(total * total, axis=-1, keepdims=True) + norm_eps)
    upstream = gain.astype(jnp.float32)[None, :] * cotangent.astype(jnp.float32)
    back = inverse * upstream - total * inverse**3 * jnp.mean(
        total * upstream, axis=-1, keepdims=True
    )
    back_low = back.astype(jnp.bfloat16)
    columns = attn
    grad = lax.psum_scatter(
        (
            lax.dot_general(
                columns, back_low, (((0,), (0,)), ((), ())), preferred_element_type=jnp.float32
            )
            * scaling
        ).astype(jnp.bfloat16),
        "fsdp",
        scatter_dimension=0,
        tiled=True,
    ).astype(jnp.float32)
    curvature = grad * epsilon / sigma
    grad_sum, curv_sum = (
        lax.psum(grad.astype(jnp.bfloat16), "sample").astype(jnp.float32),
        lax.psum(curvature.astype(jnp.bfloat16), "sample").astype(jnp.float32),
    )
    return ivon_update(mean, hess, momentum, grad_sum, curv_sum, groups)


def solution(mesh):
    placed = (
        P(),
        P(("sample", "fsdp"), None),
        P(("sample", "fsdp"), None),
        P(("sample", "fsdp"), None),
        P(),
        P("fsdp", None),
        P("fsdp", None),
        P("fsdp", None),
    )
    return jax.shard_map(
        per_device,
        mesh=mesh,
        in_specs=placed,
        out_specs=(P("fsdp", None), P("fsdp", None), P("fsdp", None)),
        check_vma=False,
    )
```

profile of v0, /device:TPU:0, one launch (start us, length us, event | category | flops | bytes accessed | tf_op | source)
XLA Modules:
  0.0 530.1 jit_solution(14531092193861123255)
XLA Ops:
  7.2 0.0 copy-start
  7.2 0.0 all-gather.2.cloned.1.call-start
  7.2 1.4 fusion.13
  8.6 5.6 %copy.14 = f32[256,4096]{0,1:T(8,128)} copy(f32[256,4096]{1,0:T(8,128)} %param.14) | data formatting | bytes 8388608 | tf_op args[6]
  14.2 5.6 %copy.19 = f32[256,4096]{0,1:T(8,128)} copy(f32[256,4096]{1,0:T(8,128)} %param.13) | data formatting | bytes 8388608 | tf_op args[5]
  20.5 7.9 %add_convert_fusion = bf16[256,4096]{0,1:T(8,128)(2,1)} fusion(f32[256,4096]{0,1:T(8,128)} %copy.14, s32[]{:T(128)} %bitcast.1, s32[]{:T(128)} %bitcast, s32[256]{0:T(256)S(1)} %add_multiply_fusion.1, f32[256,4096]{0,1:T(8,128)} %copy.19), kind=kLoop, calls=%fused_computation.22 | loop fusion | flops 36700160 | bytes 10486792 | tf_op jit(solution)/shard_map/convert_element_type | solution.py:56
  28.4 0.0 all-gather.2.cloned.1.call-update
  28.4 0.2 reduce-scatter.2.cloned.1.call-start
  28.7 6.4 %copy.15 = bf16[512,4096]{0,1:T(8,128)(2,1)} copy(bf16[512,4096]{1,0:T(8,128)(2,1)} %param.11) | data formatting | bytes 8388608 | tf_op args[3]
  35.1 6.6 %copy.12 = bf16[512,4096]{0,1:T(8,128)(2,1)} copy(bf16[512,4096]{1,0:T(8,128)(2,1)} %param.10) | data formatting | bytes 8388608 | tf_op args[2]
  41.6 141.4 %all-gather.2.cloned.1.call-done = bf16[2048,4096]{0,1:T(8,128)(2,1)} async-done(((bf16[256,4096]{0,1:T(8,128)(2,1)}), bf16[2048,4096]{0,1:T(8,128)(2,1)}) %all-gather.2.cloned.1.call-update) | async-done | bytes 16777232 | tf_op jit(solution)/shard_map/all_gather | solution.py:60
  183.1 17.4 %multiply_reduce_fusion.1 = (f32[512]{0:T(512)S(1)}, f32[512]{0:T(512)S(1)}, f32[512,4096]{0,1:T(8,128)}) fusion(bf16[512,4096]{0,1:T(8,128)(2,1)} %copy.15, f32[4096]{0:T(1024)S(1)} %convert_element_type.60, bf16[2048,4096]{0,1:T(8,128)(2,1)} %all-gather.2.cloned.1.call-done, bf16[512,2048]{1,0:T(8,128)(2,1)S(1)} %copy-done, bf16[512,4096]{0,1:T(8,128)(2,1)} %copy.12), kind=kOutput, calls=%fused_computation.6 | convolution fusion | flops 8608808960 | bytes 35672064 | tf_op jit(solution)/shard_map/dot_general | solution.py:58
  200.5 18.1 %fusion = bf16[2048,4096]{0,1:T(8,128)(2,1)} fusion(bf16[512,2048]{1,0:T(8,128)(2,1)S(1)} %copy-done, f32[512,4096]{0,1:T(8,128)} %get-tuple-element.17, bf16[512,4096]{0,1:T(8,128)(2,1)} %copy.15, f32[512]{0:T(512)S(1)} %get-tuple-element.18, f32[512]{0:T(512)S(1)} %get-tuple-element.14, f32[4096]{0:T(1024)S(1)} %convert_element_type.60, ...), kind=kOutput, calls=%fused_computation.1 | convolution fusion | flops 8621391872 | bytes 31479808 | tf_op jit(solution)/shard_map/dot_general | solution.py:73
  218.6 0.0 reduce-scatter.2.cloned.1.call-update
  218.6 0.3 all-reduce.3.cloned.1.call-start
  218.9 166.3 %reduce-scatter.2.cloned.1.call-done = bf16[256,4096]{0,1:T(8,128)(2,1)} async-done(((bf16[2048,4096]{0,1:T(8,128)(2,1)}), bf16[256,4096]{0,1:T(8,128)(2,1)}) %reduce-scatter.2.cloned.1.call-update) | async-done | bytes 2097168 | tf_op jit(solution)/shard_map/reduce_scatter | solution.py:71
  385.2 7.8 %divide_convert_fusion = bf16[256,4096]{0,1:T(8,128)(2,1)} fusion(bf16[256,4096]{0,1:T(8,128)(2,1)} %reduce-scatter.2.cloned.1.call-done, f32[256,4096]{0,1:T(8,128)} %copy.14, s32[]{:T(128)} %bitcast.1, s32[]{:T(128)} %bitcast, s32[256]{0:T(256)S(1)} %add_multiply_fusion.1), kind=kLoop, calls=%fused_computation.16 | loop fusion | flops 33554432 | bytes 8389640 | tf_op jit(solution)/shard_map/convert_element_type | solution.py:85
  393.0 0.0 all-reduce.3.cloned.1.call-update
  393.0 5.6 %copy.11 = f32[256,4096]{0,1:T(8,128)} copy(f32[256,4096]{1,0:T(8,128)} %param.15) | data formatting | bytes 8388608 | tf_op args[7]
  398.7 97.1 %all-reduce.3.cloned.1.call-done = (bf16[256,4096]{0,1:T(8,128)(2,1)}, bf16[256,4096]{0,1:T(8,128)(2,1)}) async-done(((bf16[256,4096]{0,1:T(8,128)(2,1)}, bf16[256,4096]{0,1:T(8,128)(2,1)}), (bf16[256,4096]{0,1:T(8,128)(2,1)}, bf16[256,4096]{0,1:T(8,128)(2,1)})) %all-reduce.3.cloned.1.call-update) | async-done | bytes 4194320 | tf_op jit(solution)/shard_map/psum | solution.py:85
  495.7 10.9 %divide_subtract_fusion = (f32[256,4096]{0,1:T(8,128)}, f32[256,4096]{0,1:T(8,128)}, f32[256,4096]{0,1:T(8,128)}) fusion(f32[256,4096]{0,1:T(8,128)} %copy.19, bf16[256,4096]{0,1:T(8,128)(2,1)} %get-tuple-element.9, f32[256,4096]{0,1:T(8,128)} %copy.11, f32[256,4096]{0,1:T(8,128)} %copy.14, bf16[256,4096]{0,1:T(8,128)(2,1)} %get-tuple-element.8), kind=kLoop, calls=%fused_computation.15 | loop fusion | flops 22020096 | bytes 29360128 | tf_op jit(solution)/shard_map/sub | solution.py:39
  506.6 5.6 %copy.20 = f32[256,4096]{1,0:T(8,128)} copy(f32[256,4096]{0,1:T(8,128)} %get-tuple-element.10) | data formatting | bytes 8388608
  512.2 5.6 %copy.22 = f32[256,4096]{1,0:T(8,128)} copy(f32[256,4096]{0,1:T(8,128)} %get-tuple-element.11) | data formatting | bytes 8388608
  517.8 5.7 %copy.21 = f32[256,4096]{1,0:T(8,128)} copy(f32[256,4096]{0,1:T(8,128)} %get-tuple-element.12) | data formatting | bytes 8388608
  (8 shorter events, 0.0 us)
Async XLA Ops:
  7.2 175.9 %copy-start = (bf16[512,2048]{1,0:T(8,128)(2,1)S(1)}, bf16[512,2048]{1,0:T(8,128)(2,1)}, u32[]{:S(2)}) copy-start(bf16[512,2048]{1,0:T(8,128)(2,1)} %param.9) | copy-start | bytes 6291460
  7.2 175.9 %all-gather.2.cloned.1.call-start = ((), (), s32[]{:S(2)}) async-start(), calls=%async_computation.1 | async-start | bytes 18874368 | tf_op jit(solution)/shard_map/all_gather | solution.py:60
  20.5 8.2 %copy-start.2 = (bf16[4096]{0:T(1024)(128)(2,1)S(1)}, bf16[4096]{0:T(1024)(128)(2,1)}, u32[]{:S(2)}) copy-start(bf16[4096]{0:T(1024)(128)(2,1)} %param.12) | copy-start | bytes 24580
  28.4 356.8 %reduce-scatter.2.cloned.1.call-start = ((), (), s32[]{:S(2)}) async-start(), calls=%async_computation.2 | async-start | bytes 18874368 | tf_op jit(solution)/shard_map/reduce_scatter | solution.py:71
  218.6 277.2 %all-reduce.3.cloned.1.call-start = ((), (), s32[]{:S(2)}) async-start(), calls=%async_computation.3 | async-start | bytes 8388608 | tf_op jit(solution)/shard_map/psum | solution.py:85
  517.8 5.7 %copy-start.1 = (bf16[512,2048]{1,0:T(8,128)(2,1)S(1)}, bf16[512,2048]{1,0:T(8,128)(2,1)}, u32[]{:S(2)}) copy-start(bf16[512,2048]{1,0:T(8,128)(2,1)} %param.9) | copy-start | bytes 6291460
Sparse Core Ops, SparseCore 0:
  28.5 154.5 all-gather.1
  218.7 166.4 reduce-scatter.1
  393.2 102.5 all-reduce.2
where the time goes:
time: 531 us; the launch traced here: 530 us
  waiting for transfers between devices  405 us (76%)
  local copies, waits for them, and re-layouts  48.1 us (9%)
  matrix products  35.5 us (7%)
  other arithmetic  26.6 us (5%)
  between operations  14.4 us (3%)
    reduce_scatter x1, waiting for transfers between devices, per_device(): lax.psum_scatter((lax.dot_general(columns, back_low, (((0,), (0,)), ((),...  166 us
    all_gather x1, waiting for transfers between devices, per_device(): lax.all_gather(sampled, 'fsdp', axis=0, tiled=True)  141 us
    psum x1, waiting for transfers between devices, per_device(): lax.psum(curvature.astype(jnp.bfloat16), 'sample').astype(jnp.float32)  97.1 us
    unnamed x14, local copies, waits for them, and re-layouts  46.7 us
    dot_general x1, matrix products, per_device(): lax.dot_general(columns, back_low, (((0,), (0,)), ((), ())), preferred_el...  18.1 us
    dot_general x1, matrix products, per_device(): jnp.dot(columns, lax.all_gather(sampled, 'fsdp', axis=0, tiled=True), pre...  17.4 us
    sub x1, other arithmetic, ivon_update(): mean - step_size * (new_momentum + damping * mean) / (new_hess + damping)  10.9 us
  transfers between devices with their start and end apart: 3, of which 3 were waited for; matrix products, arithmetic and copies ran while one was open for 4% of the time, Pallas kernels for 0%

commit v1 on v0

--- a/solution.py
+++ b/solution.py
@@ -82,7 +82,9 @@
     curvature = grad * epsilon / sigma
     grad_sum, curv_sum = (
         lax.psum(grad.astype(jnp.bfloat16), "sample").astype(jnp.float32),
-        lax.psum(curvature.astype(jnp.bfloat16), "sample").astype(jnp.float32),
+        jnp.sum(lax.all_gather(curvature.astype(jnp.bfloat16), "sample"), axis=0).astype(
+            jnp.float32
+        ),
     )
     return ivon_update(mean, hess, momentum, grad_sum, curv_sum, groups)
 

time: 531 us -> 586 us (1.10)
  waiting for transfers between devices: 405 us -> 425 us
  other arithmetic: 26.6 us -> 46.4 us
  local copies, waits for them, and re-layouts: 48.1 us -> 62.8 us
    all_gather x0 -> x1, waiting for transfers between devices: none -> 79.8 us  [per_device(): lax.all_gather(curvature.astype(jnp.bfloat16), 'sample')]
    psum x1, waiting for transfers between devices: 97.1 us -> 36.9 us  [per_device(): lax.psum(grad.astype(jnp.bfloat16), 'sample').astype(jnp.float32)]
    reduce_sum x0 -> x1, other arithmetic: none -> 21.1 us  [per_device(): jnp.sum(lax.all_gather(curvature.astype(jnp.bfloat16), 'sample'), axis=0)]
    all_gather x0 -> x1, local copies, waits for them, and re-layouts: none -> 14.7 us  [per_device(): lax.all_gather(curvature.astype(jnp.bfloat16), 'sample')]
  transfers between devices with their start and end apart: 3 -> 4, of which waited for: 3 -> 4; matrix products, arithmetic and copies ran while one was open for 4% -> 9% of each run, Pallas kernels for 0% -> 0%
where the time goes in v1:
time: 586 us; the launch traced here: 585 us
  waiting for transfers between devices  425 us (73%)
  local copies, waits for them, and re-layouts  62.8 us (11%)
  other arithmetic  46.4 us (8%)
  matrix products  35.5 us (6%)
  between operations  14.5 us (2%)
    reduce_scatter x1, waiting for transfers between devices, per_device(): lax.psum_scatter((lax.dot_general(columns, back_low, (((0,), (0,)), ((),...  166 us
    all_gather x1, waiting for transfers between devices, per_device(): lax.all_gather(sampled, 'fsdp', axis=0, tiled=True)  141 us
    all_gather x1, waiting for transfers between devices, per_device(): lax.all_gather(curvature.astype(jnp.bfloat16), 'sample')  79.8 us
    unnamed x14, local copies, waits for them, and re-layouts  46.7 us
    psum x1, waiting for transfers between devices, per_device(): lax.psum(grad.astype(jnp.bfloat16), 'sample').astype(jnp.float32)  36.9 us
    reduce_sum x1, other arithmetic, per_device(): jnp.sum(lax.all_gather(curvature.astype(jnp.bfloat16), 'sample'), axis=0)  21.1 us
    dot_general x1, matrix products, per_device(): lax.dot_general(columns, back_low, (((0,), (0,)), ((), ())), preferred_el...  18.1 us
    dot_general x1, matrix products, per_device(): jnp.dot(columns, lax.all_gather(sampled, 'fsdp', axis=0, tiled=True), pre...  17.4 us
  transfers between devices with their start and end apart: 4, of which 4 were waited for; matrix products, arithmetic and copies ran while one was open for 9% of the time, Pallas kernels for 0%

profile of v1, /device:TPU:0, one launch (start us, length us, event | category | flops | bytes accessed | tf_op | source)
XLA Modules:
  0.0 584.7 jit_solution(327330280234315102)
XLA Ops:
  7.2 1.4 fusion.13
  8.6 5.6 copy.14
  14.2 5.6 copy.19
  20.5 8.0 %add_convert_fusion = bf16[256,4096]{0,1:T(8,128)(2,1)} fusion(f32[256,4096]{0,1:T(8,128)} %copy.14, s32[]{:T(128)} %bitcast.1, s32[]{:T(128)} %bitcast, s32[256]{0:T(256)S(1)} %add_multiply_fusion.1, f32[256,4096]{0,1:T(8,128)} %copy.19), kind=kLoop, calls=%fused_computation.22 | loop fusion | flops 36700160 | bytes 10486792 | tf_op jit(solution)/shard_map/convert_element_type | solution.py:56
  28.5 0.2 reduce-scatter.2.cloned.1.call-start
  28.7 6.4 %copy.15 = bf16[512,4096]{0,1:T(8,128)(2,1)} copy(bf16[512,4096]{1,0:T(8,128)(2,1)} %param.11) | data formatting | bytes 8388608 | tf_op args[3]
  35.1 6.6 %copy.12 = bf16[512,4096]{0,1:T(8,128)(2,1)} copy(bf16[512,4096]{1,0:T(8,128)(2,1)} %param.10) | data formatting | bytes 8388608 | tf_op args[2]
  41.7 141.4 %all-gather.4.cloned.1.call-done = bf16[2048,4096]{0,1:T(8,128)(2,1)} async-done(((bf16[256,4096]{0,1:T(8,128)(2,1)}), bf16[2048,4096]{0,1:T(8,128)(2,1)}) %all-gather.4.cloned.1.call-update) | async-done | bytes 16777232 | tf_op jit(solution)/shard_map/all_gather | solution.py:60
  183.2 17.4 %multiply_reduce_fusion.1 = (f32[512]{0:T(512)S(1)}, f32[512]{0:T(512)S(1)}, f32[512,4096]{0,1:T(8,128)}) fusion(bf16[512,4096]{0,1:T(8,128)(2,1)} %copy.15, f32[4096]{0:T(1024)S(1)} %convert_element_type.62, bf16[2048,4096]{0,1:T(8,128)(2,1)} %all-gather.4.cloned.1.call-done, bf16[512,2048]{1,0:T(8,128)(2,1)S(1)} %copy-done, bf16[512,4096]{0,1:T(8,128)(2,1)} %copy.12), kind=kOutput, calls=%fused_computation.6 | convolution fusion | flops 8608808960 | bytes 35672064 | tf_op jit(solution)/shard_map/dot_general | solution.py:58
  200.6 18.1 %fusion = bf16[2048,4096]{0,1:T(8,128)(2,1)} fusion(bf16[512,2048]{1,0:T(8,128)(2,1)S(1)} %copy-done, f32[512,4096]{0,1:T(8,128)} %get-tuple-element.15, bf16[512,4096]{0,1:T(8,128)(2,1)} %copy.15, f32[512]{0:T(512)S(1)} %get-tuple-element.16, f32[512]{0:T(512)S(1)} %get-tuple-element.12, f32[4096]{0:T(1024)S(1)} %convert_element_type.62, ...), kind=kOutput, calls=%fused_computation.1 | convolution fusion | flops 8621391872 | bytes 31479808 | tf_op jit(solution)/shard_map/dot_general | solution.py:73
  218.7 0.3 all-gather.6.cloned.1.call-start
  218.9 166.3 %reduce-scatter.2.cloned.1.call-done = bf16[256,4096]{0,1:T(8,128)(2,1)} async-done(((bf16[2048,4096]{0,1:T(8,128)(2,1)}), bf16[256,4096]{0,1:T(8,128)(2,1)}) %reduce-scatter.2.cloned.1.call-update) | async-done | bytes 2097168 | tf_op jit(solution)/shard_map/reduce_scatter | solution.py:71
  385.2 7.9 %divide_convert_fusion = bf16[256,4096]{0,1:T(8,128)(2,1)} fusion(bf16[256,4096]{0,1:T(8,128)(2,1)} %reduce-scatter.2.cloned.1.call-done, f32[256,4096]{0,1:T(8,128)} %copy.14, s32[]{:T(128)} %bitcast.1, s32[]{:T(128)} %bitcast, s32[256]{0:T(256)S(1)} %add_multiply_fusion.1), kind=kLoop, calls=%fused_computation.16 | loop fusion | flops 33554432 | bytes 8389640 | tf_op jit(solution)/shard_map/convert_element_type | solution.py:85
  393.2 0.0 all-reduce.2.cloned.1.call-start
  393.2 0.5 all-reduce.2.cloned.1.call-update
  393.7 5.6 copy.11
  399.3 79.8 %all-gather.6.cloned.1.call-done = bf16[1024,4096]{0,1:T(8,128)(2,1)} async-done(((bf16[256,4096]{0,1:T(8,128)(2,1)}), bf16[1024,4096]{0,1:T(8,128)(2,1)}) %all-gather.6.cloned.1.call-update) | async-done | bytes 8388624 | tf_op jit(solution)/shard_map/all_gather | solution.py:85
  479.1 14.7 %reshape.36 = bf16[4,256,4096]{1,0,2:T(4,128)(2,1)} reshape(bf16[1024,4096]{0,1:T(8,128)(2,1)} %all-gather.6.cloned.1.call-done) | data formatting | bytes 16777216 | tf_op jit(solution)/shard_map/all_gather | solution.py:85
  493.8 21.1 %reduce_sum.32 = bf16[256,4096]{0,1:T(8,128)(2,1)S(1)} reduce(bf16[4,256,4096]{1,0,2:T(4,128)(2,1)} %reshape.36, bf16[]{:T(256)} %constant.71.clone.1), dimensions={0}, to_apply=%region_4.0 | reduce | flops 3145728 | bytes 10485762 | tf_op jit(solution)/shard_map/reduce_sum | solution.py:85
  515.0 36.9 %all-reduce.2.cloned.1.call-done = bf16[256,4096]{0,1:T(8,128)(2,1)} async-done(((bf16[256,4096]{0,1:T(8,128)(2,1)}), bf16[256,4096]{0,1:T(8,128)(2,1)}) %all-reduce.2.cloned.1.call-update) | async-done | bytes 2097168 | tf_op jit(solution)/shard_map/psum | solution.py:84
  551.8 9.4 %divide_subtract_fusion = (f32[256,4096]{0,1:T(8,128)}, f32[256,4096]{0,1:T(8,128)}, f32[256,4096]{0,1:T(8,128)}) fusion(f32[256,4096]{0,1:T(8,128)} %copy.19, bf16[256,4096]{0,1:T(8,128)(2,1)} %all-reduce.2.cloned.1.call-done, f32[256,4096]{0,1:T(8,128)} %copy.11, f32[256,4096]{0,1:T(8,128)} %copy.14, bf16[256,4096]{0,1:T(8,128)(2,1)S(1)} %reduce_sum.32), kind=kLoop, calls=%fused_computation.15 | loop fusion | flops 22020096 | bytes 29360128 | tf_op jit(solution)/shard_map/sub | solution.py:39
  561.2 5.6 copy.20
  566.8 5.6 copy.22
  572.4 5.7 copy.21
  (13 shorter events, 0.1 us)
Async XLA Ops:
  7.2 176.0 %copy-start = (bf16[512,2048]{1,0:T(8,128)(2,1)S(1)}, bf16[512,2048]{1,0:T(8,128)(2,1)}, u32[]{:S(2)}) copy-start(bf16[512,2048]{1,0:T(8,128)(2,1)} %param.9) | copy-start | bytes 6291460
  7.2 176.0 %all-gather.4.cloned.1.call-start = ((), (), s32[]{:S(2)}) async-start(), calls=%async_computation.1 | async-start | bytes 18874368 | tf_op jit(solution)/shard_map/all_gather | solution.py:60
  20.5 8.2 %copy-start.2 = (bf16[4096]{0:T(1024)(128)(2,1)S(1)}, bf16[4096]{0:T(1024)(128)(2,1)}, u32[]{:S(2)}) copy-start(bf16[4096]{0:T(1024)(128)(2,1)} %param.12) | copy-start | bytes 24580
  28.5 356.8 %reduce-scatter.2.cloned.1.call-start = ((), (), s32[]{:S(2)}) async-start(), calls=%async_computation.2 | async-start | bytes 18874368 | tf_op jit(solution)/shard_map/reduce_scatter | solution.py:71
  218.7 260.5 %all-gather.6.cloned.1.call-start = ((), (), s32[]{:S(2)}) async-start(), calls=%async_computation.4 | async-start | bytes 10485760 | tf_op jit(solution)/shard_map/all_gather | solution.py:85
  393.2 158.7 %all-reduce.2.cloned.1.call-start = ((), (), s32[]{:S(2)}) async-start(), calls=%async_computation.3 | async-start | bytes 4194304 | tf_op jit(solution)/shard_map/psum | solution.py:84
  572.4 5.7 copy-start.1
Sparse Core Ops, SparseCore 0:
  28.6 154.5 all-gather.3
  218.8 166.4 reduce-scatter.1
  393.3 85.8 all-gather.5
  482.1 69.6 all-reduce.1
